TPU v7x, 512 devices: a whole 4x4x16 slice. The times are simulated.
512 devices in a mesh: replica: 64 (over y, z_lo, core), tensor: 8 (over z_hi, x).
Axes of the slice: x: 4, y: 4, z: 16 (z_hi: 2, z_lo: 8; z = z_hi * 8 + z_lo), core: 2. Of those that a mesh axis runs over, the one named last changes fastest.
Arguments:
- hidden_act: bfloat16 [16384, 7168], P('replica', 'tensor'), may hold values from -15 to 15
- residual_in: bfloat16 [512, 65536], P('tensor', 'replica'), may hold values from -6 to 6
- cotangent: bfloat16 [512, 65536], P('tensor', 'replica'), may hold values from -6 to 6
- norm_gain: bfloat16 [2048], replicated, may hold values from 0.25 to 1.75
- inner_weight: bfloat16 [7168, 65536], P('tensor', 'replica'), may hold values from -24 to 24
- anchor: bfloat16 [7168, 2048], P('tensor', 'replica'), may hold values from -6 to 6
- momentum: bfloat16 [7168, 2048], P('tensor', 'replica'), may hold values from -3 to 3
Outputs:
- normed: bfloat16 [512, 65536], P('tensor', 'replica')
- mixed_weight: bfloat16 [7168, 65536], P('tensor', 'replica')
- momentum_out: bfloat16 [7168, 2048], P('tensor', 'replica')
All inputs are finite; a program needn't handle non-finite values.
Results may differ from a plain program's by a relative error of at most 0.0075.
Values may be sent and summed in bfloat16 or wider, within the bound.
A program may use at most 64 MiB of HBM per device.

v0:
```python
import math
import jax
import jax.numpy as jnp
from jax import lax
from jax.sharding import PartitionSpec as P

FF = 7168
TOK = 512
inner_rate = 0.2
outer_rate = 0.7
outer_mu = 0.9
mix_share = 0.5


def partner(array, axis, stride):
    return lax.ppermute(array, axis, [(i, i ^ 1 << stride) for i in range(lax.axis_size(axis))])


def norm_rows(out_rows, resid_rows, cot_rows, norm_scale, total_features):
    summed_in = resid_rows.astype(jnp.float32) + out_rows
    dz_rows = cot_rows.astype(jnp.float32) * norm_scale
    own_squares = jnp.sum(summed_in * summed_in, axis=-1)
    own_cross = jnp.sum(dz_rows * summed_in, axis=-1)
    other_squares, other_cross = partner((own_squares, own_cross), "replica", 0)
    mean_squares = ((own_squares + other_squares) / total_features)[:, None]
    inner_mean = ((own_cross + other_cross) / total_features)[:, None]
    root_inv = lax.rsqrt(mean_squares + 1e-05)
    normed = (summed_in * root_inv * norm_scale).astype(jnp.bfloat16)
    slopes = (root_inv * (dz_rows - summed_in * inner_mean * root_inv * root_inv)).astype(
        jnp.bfloat16
    )
    return (normed, slopes)


def local(hidden_act, residual_in, cotangent, norm_gain, inner_weight, anchor, momentum):
    ff_local = inner_weight.shape[0]
    half_cols = inner_weight.shape[1]
    total_features = 2 * half_cols
    multiplier = 1.0 / math.sqrt(FF)
    step_scale = inner_rate * math.sqrt(FF / TOK)
    side = lax.axis_index("replica") % 2
    first = side == 0
    norm_scale = lax.dynamic_slice_in_dim(norm_gain, side * half_cols, half_cols, 0).astype(
        jnp.float32
    )
    partner_rows = partner(hidden_act, "replica", 0)
    hidden_full = jnp.where(
        first,
        jnp.concatenate([hidden_act, partner_rows], 0),
        jnp.concatenate([partner_rows, hidden_act], 0),
    )
    contract = (((0,), (0,)), ((), ()))
    row_block = hidden_full
    out_rows = lax.psum_scatter(
        jnp.dot(row_block, inner_weight, preferred_element_type=jnp.float32) * multiplier,
        "tensor",
        scatter_dimension=0,
        tiled=True,
    )
    normed, slopes = norm_rows(out_rows, residual_in, cotangent, norm_scale, total_features)
    row_block = hidden_full
    gradient = lax.dot_general(
        row_block,
        lax.all_gather(slopes, "tensor", axis=0, tiled=True),
        contract,
        preferred_element_type=jnp.float32,
    )
    gradient = gradient * multiplier
    stepped = inner_weight.astype(jnp.float32) - step_scale * gradient
    replica_count = lax.axis_size("replica") // 2
    buffer = jnp.zeros((1, ff_local, total_features), jnp.bfloat16)
    buffer = lax.dynamic_update_slice(buffer, inner_weight[None], (0, 0, side * half_cols))
    received = lax.all_to_all(buffer, "replica", split_axis=2, concat_axis=0, tiled=True)
    summed = jnp.sum(received, axis=0, dtype=jnp.float32)
    anchor_f = anchor.astype(jnp.float32)
    pseudo = anchor_f - summed / replica_count
    moment = (outer_mu * momentum.astype(jnp.float32) + pseudo).astype(jnp.bfloat16)
    new_anchor = (anchor_f - outer_rate * (pseudo + outer_mu * moment.astype(jnp.float32))).astype(
        jnp.bfloat16
    )
    full_anchor = lax.all_gather(new_anchor, "replica", axis=1, tiled=True)
    own_anchor = lax.dynamic_slice_in_dim(full_anchor, side * half_cols, half_cols, 1)
    mixed = (mix_share * stepped + (1.0 - mix_share) * own_anchor.astype(jnp.float32)).astype(
        jnp.bfloat16
    )
    return (normed, mixed, moment)


def solution(mesh):
    in_specs = (
        P("replica", "tensor"),
        P("tensor", "replica"),
        P("tensor", "replica"),
        P(),
        P("tensor", "replica"),
        P("tensor", "replica"),
        P("tensor", "replica"),
    )
    out_specs = (P("tensor", "replica"), P("tensor", "replica"), P("tensor", "replica"))
    return jax.shard_map(local, mesh=mesh, in_specs=in_specs, out_specs=out_specs, check_vma=False)
```

profile of v0, /device:TPU:8, one launch (start us, length us, event | category | flops | bytes accessed | tf_op | source)
XLA Modules:
  0.0 599.8 jit_solution(8487567397777229452)
XLA Ops:
  8.0 9.8 %copy.20 = bf16[1,896,1024]{1,0,2:T(2,128)(2,1)} copy(bf16[1,896,1024]{2,1,0:T(8,128)(2,1)} %bitcast.9) | data formatting | bytes 3670016 | tf_op jit(solution)/shard_map/broadcast_in_dim | solution.py:72
  17.8 4.9 broadcast_in_dim.4
  22.7 5.6 constant_dynamic-update-slice_fusion
  28.8 79.9 %reduce.3 = bf16[2048,896]{1,0:T(8,128)(2,1)} reduce(bf16[2048,1,896]{2,1,0:T(2,128)(2,1)} %bitcast.3, bf16[]{:T(256)} %broadcast.27), dimensions={1}, to_apply=%bitcast.3.reduce_sub_computation | reduce | bytes 7340034
  108.7 8.3 %reshape.16 = bf16[64,2,14336]{2,1,0:T(2,128)(2,1)} reshape(bf16[2048,896]{1,0:T(8,128)(2,1)} %reduce.3) | data formatting | bytes 7340032
  117.0 16.5 %all-to-all-start = ((bf16[64,2,14336]{2,1,0:T(2,128)(2,1)}), bf16[64,2,14336]{2,1,0:T(2,128)(2,1)}, u32[]{:S(2)}, u32[]{:S(2)}) async-start(bf16[64,2,14336]{2,1,0:T(2,128)(2,1)} %reshape.16), calls=%async_computation.1 | async-start | bytes 7340032 | tf_op jit(solution)/shard_map/all_to_all | solution.py:73
  133.5 2.1 collective-permute-start
  135.6 1.6 collective-permute-done
  137.2 2.6 convolution_multiply_fusion
  139.9 209.9 %all-to-all-done = bf16[64,2,14336]{2,1,0:T(2,128)(2,1)} async-done(((bf16[64,2,14336]{2,1,0:T(2,128)(2,1)}), bf16[64,2,14336]{2,1,0:T(2,128)(2,1)}, u32[]{:S(2)}, u32[]{:S(2)}) %all-to-all-start) | async-done | bytes 3670048 | tf_op jit(solution)/shard_map/all_to_all | solution.py:73
  349.9 19.3 %reshape.17 = bf16[2048,1,896]{2,1,0:T(2,128)(2,1)} reshape(bf16[64,2,14336]{2,1,0:T(2,128)(2,1)} %all-to-all-done) | data formatting | bytes 7340032
  369.2 3.7 copy.21
  372.9 0.5 convert_reduce_fusion
  373.7 0.7 fusion
  374.6 1.1 multiply_reduce_fusion
  375.7 4.9 collective-permute-start.1
  380.6 1.9 collective-permute-start.2
  382.6 1.1 collective-permute-done.2
  383.7 1.8 multiply_convert_fusion.1
  385.5 110.6 %all-gather.5.cloned.1.call-done = bf16[896,2048]{0,1:T(8,128)(2,1)} async-done(((bf16[896,32]{0,1:T(8,128)(2,1)}), bf16[896,2048]{0,1:T(8,128)(2,1)}) %all-gather.5.cloned.1.call-update) | async-done | bytes 3670032 | tf_op jit(solution)/shard_map/all_gather | solution.py:81
  496.1 1.6 constant_dynamic-slice_fusion
  497.7 2.4 copy.23
  500.1 87.1 %all-gather.3.cloned.1.call-done = bf16[512,1024]{1,0:T(8,128)(2,1)} async-done(((bf16[64,1024]{1,0:T(8,128)(2,1)}), bf16[512,1024]{1,0:T(8,128)(2,1)}) %all-gather.3.cloned.1.call-update) | async-done | bytes 1048592 | tf_op jit(solution)/shard_map/all_gather | solution.py:64
  587.2 5.1 multiply_convert_fusion
  (28 shorter events, 1.0 us)
Async XLA Ops:
  17.8 4.9 copy-start
  117.0 16.5 %copy-start.7 = (bf16[256,896]{1,0:T(8,128)(2,1)S(1)}, bf16[256,896]{1,0:T(8,128)(2,1)}, u32[]{:S(2)}) copy-start(bf16[256,896]{1,0:T(8,128)(2,1)} %param.7) | copy-start | bytes 1376260
  117.0 20.2 %copy-start.1 = (bf16[896,1024]{1,0:T(8,128)(2,1)S(1)}, bf16[896,1024]{1,0:T(8,128)(2,1)}, u32[]{:S(2)}) copy-start(bf16[896,1024]{1,0:T(8,128)(2,1)} %param.11) | copy-start | bytes 5505028
  117.0 232.9 %all-to-all-start = ((bf16[64,2,14336]{2,1,0:T(2,128)(2,1)}), bf16[64,2,14336]{2,1,0:T(2,128)(2,1)}, u32[]{:S(2)}, u32[]{:S(2)}) async-start(bf16[64,2,14336]{2,1,0:T(2,128)(2,1)} %reshape.16), calls=%async_computation.1 | async-start | bytes 7340032 | tf_op jit(solution)/shard_map/all_to_all | solution.py:73
  133.5 241.1 %reduce-scatter.2.cloned.1.call-start = ((), (), s32[]{:S(2)}) async-start(), calls=%async_computation.2 | async-start | bytes 2359296 | tf_op jit(solution)/shard_map/reduce_scatter | solution.py:54
  133.5 3.7 collective-permute-start
  139.9 356.2 %all-gather.5.cloned.1.call-start = ((), (), s32[]{:S(2)}) async-start(), calls=%async_computation.4 | async-start | bytes 3727360 | tf_op jit(solution)/shard_map/all_gather | solution.py:81
  372.9 0.8 copy-start.4
  372.9 0.8 copy-start.5
  372.9 1.6 copy-start.6
  372.9 1.6 copy-start.2
  372.9 1.6 copy-start.3
  374.4 212.8 %all-gather.3.cloned.1.call-start = ((), (), s32[]{:S(2)}) async-start(), calls=%async_computation.3 | async-start | bytes 1179648 | tf_op jit(solution)/shard_map/all_gather | solution.py:64
  375.7 6.9 %collective-permute-start.1 = (f32[64]{0:T(128)S(1)}, f32[64]{0:T(128)S(1)}, u32[]{:S(2)}, u32[]{:S(2)}) collective-permute-start(f32[64]{0:T(128)S(1)} %get-tuple-element.10), channel_id=1, source_target_pairs={{0,8},{8,0},{16,24},{24,16},{32,40},{40,32},{48,56},{56,48},{64,72... | collective-permute-start | bytes 776 | tf_op jit(solution)/shard_map/ppermute | solution.py:16
  380.6 3.0 collective-permute-start.2
Sparse Core Ops, SparseCore 0:
  140.0 208.6 reduce-scatter.1
Sparse Core Ops, SparseCore 1:
  374.5 121.5 all-gather.4
  499.6 87.5 all-gather.2
where the time goes:
time: 601 us; the launch traced here: 600 us
  waiting for transfers between devices  410 us (68%)
  other arithmetic  84 us (14%)
  local copies, waits for them, and re-layouts  56.4 us (9%)
  starting transfers between devices  25.5 us (4%)
  between operations  15.7 us (3%)
  matrix products  7.78 us (1%)
    all_to_all x1, waiting for transfers between devices, local(): lax.all_to_all(buffer, 'replica', split_axis=2, concat_axis=0, tiled=True)  210 us
    all_gather x1, waiting for transfers between devices, local(): full_anchor = lax.all_gather(new_anchor, 'replica', axis=1, tiled=True)  111 us
    all_gather x1, waiting for transfers between devices, local(): lax.all_gather(slopes, 'tensor', axis=0, tiled=True)  87.1 us
    unnamed x1, other arithmetic  79.9 us
    unnamed x20, local copies, waits for them, and re-layouts  30.9 us
    all_to_all x1, starting transfers between devices, local(): lax.all_to_all(buffer, 'replica', split_axis=2, concat_axis=0, tiled=True)  16.5 us
  transfers between devices with their start and end apart: 7, of which 5 were waited for; matrix products, arithmetic and copies ran while one was open for 6% of the time, Pallas kernels for 0%

commit v1 on v0

--- a/solution.py
+++ b/solution.py
@@ -78,7 +78,10 @@
     new_anchor = (anchor_f - outer_rate * (pseudo + outer_mu * moment.astype(jnp.float32))).astype(
         jnp.bfloat16
     )
-    full_anchor = lax.all_gather(new_anchor, "replica", axis=1, tiled=True)
+    count = lax.axis_size("replica")
+    blocks = jnp.stack([new_anchor for _ in range(count)])
+    blocks = lax.all_to_all(blocks, "replica", split_axis=0, concat_axis=0)
+    full_anchor = jnp.concatenate(blocks, axis=1)
     own_anchor = lax.dynamic_slice_in_dim(full_anchor, side * half_cols, half_cols, 1)
     mixed = (mix_share * stepped + (1.0 - mix_share) * own_anchor.astype(jnp.float32)).astype(
         jnp.bfloat16

time: 601 us -> 661 us (1.100)
  blocking collectives: 0 us -> 179 us
  waiting for transfers between devices: 410 us -> 300 us
  starting transfers between devices: 25.5 us -> 16.1 us
    all_to_all x1, waiting for transfers between devices: 210 us -> 0.01 us  [local(): blocks = lax.all_to_all(blocks, 'replica', split_axis=0, concat_axis=0)]
    reduce_scatter x1, waiting for transfers between devices: 0.02 us -> 208 us  [local(): lax.psum_scatter(jnp.dot(row_block, inner_weight, preferred_element_type=...]
    all_to_all x0 -> x1, blocking collectives: none -> 179 us  [local(): lax.all_to_all(buffer, 'replica', split_axis=2, concat_axis=0, tiled=True)]
    all_gather x1 -> x0, waiting for transfers between devices: 111 us -> none  [local(): full_anchor = lax.all_gather(new_anchor, 'replica', axis=1, tiled=True)]
    all_to_all x1, starting transfers between devices: 16.5 us -> 9.67 us  [local(): blocks = lax.all_to_all(blocks, 'replica', split_axis=0, concat_axis=0)]
  transfers between devices with their start and end apart: 7 -> 6, of which waited for: 5 -> 4; matrix products, arithmetic and copies ran while one was open for 6% -> 1% of each run, Pallas kernels for 0% -> 0%
where the time goes in v1:
time: 661 us; the launch traced here: 660 us
  waiting for transfers between devices  300 us (45%)
  blocking collectives  179 us (27%)
  other arithmetic  84 us (13%)
  local copies, waits for them, and re-layouts  59.1 us (9%)
  starting transfers between devices  16.1 us (2%)
  between operations  14.2 us (2%)
  matrix products  7.78 us (1%)
    reduce_scatter x1, waiting for transfers between devices, local(): lax.psum_scatter(jnp.dot(row_block, inner_weight, preferred_element_type=...  208 us
    all_to_all x1, blocking collectives, local(): lax.all_to_all(buffer, 'replica', split_axis=2, concat_axis=0, tiled=True)  179 us
    all_gather x1, waiting for transfers between devices, local(): lax.all_gather(slopes, 'tensor', axis=0, tiled=True)  89.2 us
    unnamed x1, other arithmetic  79.8 us
    unnamed x20, local copies, waits for them, and re-layouts  31.5 us
  transfers between devices with their start and end apart: 6, of which 4 were waited for; matrix products, arithmetic and copies ran while one was open for 1% of the time, Pallas kernels for 0%

profile of v1, /device:TPU:8, one launch (start us, length us, event | category | flops | bytes accessed | tf_op | source)
XLA Modules:
  0.0 659.6 jit_solution(17404095857106054309)
XLA Ops:
  7.2 9.7 %copy.16 = bf16[1,896,1024]{1,0,2:T(2,128)(2,1)} copy(bf16[1,896,1024]{2,1,0:T(8,128)(2,1)} %bitcast.12) | data formatting | bytes 3670016 | tf_op jit(solution)/shard_map/broadcast_in_dim | solution.py:72
  16.9 4.9 broadcast_in_dim.4
  21.8 5.6 constant_dynamic-update-slice_fusion
  27.9 79.8 %reduce.3 = bf16[2048,896]{1,0:T(8,128)(2,1)} reduce(bf16[2048,1,896]{2,1,0:T(2,128)(2,1)} %bitcast.6, bf16[]{:T(256)} %broadcast.29), dimensions={1}, to_apply=%bitcast.6.reduce_sub_computation | reduce | bytes 7340034
  107.7 8.3 %reshape.26 = bf16[64,2,14336]{2,1,0:T(2,128)(2,1)} reshape(bf16[2048,896]{1,0:T(8,128)(2,1)} %reduce.3) | data formatting | bytes 7340032
  116.0 178.7 %all_to_all.14 = bf16[64,2,14336]{2,1,0:T(2,128)(2,1)} all-to-all(bf16[64,2,14336]{2,1,0:T(2,128)(2,1)} %reshape.26), channel_id=1, replica_groups=mesh['replica'=64,'tensor'=8] {'replica'}, dimensions={0} | all-to-all | bytes 7340032 | tf_op jit(solution)/shard_map/all_to_all | solution.py:73
  294.7 19.3 %reshape.27 = bf16[2048,1,896]{2,1,0:T(2,128)(2,1)} reshape(bf16[64,2,14336]{2,1,0:T(2,128)(2,1)} %all_to_all.14) | data formatting | bytes 7340032
  314.0 3.7 copy.17
  318.6 0.7 fusion
  319.2 2.1 stack.2
  321.3 9.7 %all-to-all-start.1 = ((bf16[64,896,32]{1,2,0:T(8,128)(2,1)}), bf16[64,896,32]{1,2,0:T(8,128)(2,1)}, u32[]{:S(2)}, u32[]{:S(2)}) async-start(bf16[64,896,32]{1,2,0:T(8,128)(2,1)} %stack.2), calls=%async_computation.2 | async-start | bytes 7340032 | tf_op jit(solution)/shard_map/all_to_all | solution.py:83
  331.1 2.1 collective-permute-start
  333.1 1.6 collective-permute-done
  334.8 2.6 convolution_multiply_fusion
  338.1 208.1 %reduce-scatter.2.cloned.1.call-done = f32[64,1024]{1,0:T(8,128)} async-done(((f32[512,1024]{1,0:T(8,128)}), f32[64,1024]{1,0:T(8,128)}) %reduce-scatter.2.cloned.1.call-update) | async-done | bytes 262160 | tf_op jit(solution)/shard_map/reduce_scatter | solution.py:54
  546.2 1.1 multiply_reduce_fusion
  547.4 1.9 collective-permute-start.1
  549.3 2.4 collective-permute-start.2
  551.7 0.8 collective-permute-done.2
  552.5 1.8 multiply_convert_fusion.1
  554.3 1.7 constant_dynamic-slice_fusion
  556.0 2.4 copy.19
  558.4 89.2 %all-gather.2.cloned.1.call-done = bf16[512,1024]{1,0:T(8,128)(2,1)} async-done(((bf16[64,1024]{1,0:T(8,128)(2,1)}), bf16[512,1024]{1,0:T(8,128)(2,1)}) %all-gather.2.cloned.1.call-update) | async-done | bytes 1048592 | tf_op jit(solution)/shard_map/all_gather | solution.py:64
  647.6 5.1 multiply_convert_fusion
  (27 shorter events, 2.1 us)
Async XLA Ops:
  16.9 4.9 copy-start
  317.7 0.8 copy-start.4
  317.7 0.8 copy-start.5
  321.3 9.7 %copy-start.7 = (bf16[256,896]{1,0:T(8,128)(2,1)S(1)}, bf16[256,896]{1,0:T(8,128)(2,1)}, u32[]{:S(2)}) copy-start(bf16[256,896]{1,0:T(8,128)(2,1)} %param.7) | copy-start | bytes 1376260
  321.3 13.4 %copy-start.1 = (bf16[896,1024]{1,0:T(8,128)(2,1)S(1)}, bf16[896,1024]{1,0:T(8,128)(2,1)}, u32[]{:S(2)}) copy-start(bf16[896,1024]{1,0:T(8,128)(2,1)} %param.11) | copy-start | bytes 5505028
  321.3 233.0 %all-to-all-start.1 = ((bf16[64,896,32]{1,2,0:T(8,128)(2,1)}), bf16[64,896,32]{1,2,0:T(8,128)(2,1)}, u32[]{:S(2)}, u32[]{:S(2)}) async-start(bf16[64,896,32]{1,2,0:T(8,128)(2,1)} %stack.2), calls=%async_computation.2 | async-start | bytes 7340032 | tf_op jit(solution)/shard_map/all_to_all | solution.py:83
  331.0 215.2 %reduce-scatter.2.cloned.1.call-start = ((), (), s32[]{:S(2)}) async-start(), calls=%async_computation.3 | async-start | bytes 2359296 | tf_op jit(solution)/shard_map/reduce_scatter | solution.py:54
  331.1 3.7 collective-permute-start
  337.4 0.7 copy-start.6
  337.4 208.8 %copy-start.2 = (bf16[64,1024]{1,0:T(8,128)(2,1)S(1)}, bf16[64,1024]{1,0:T(8,128)(2,1)}, u32[]{:S(2)}) copy-start(bf16[64,1024]{1,0:T(8,128)(2,1)} %param.9) | copy-start | bytes 393220
  337.4 208.8 %copy-start.3 = (bf16[64,1024]{1,0:T(8,128)(2,1)S(1)}, bf16[64,1024]{1,0:T(8,128)(2,1)}, u32[]{:S(2)}) copy-start(bf16[64,1024]{1,0:T(8,128)(2,1)} %param.8) | copy-start | bytes 393220
  337.5 310.1 %all-gather.2.cloned.1.call-start = ((), (), s32[]{:S(2)}) async-start(), calls=%async_computation.4 | async-start | bytes 1179648 | tf_op jit(solution)/shard_map/all_gather | solution.py:64
  547.4 4.3 collective-permute-start.1
  549.3 3.2 collective-permute-start.2
Sparse Core Ops, SparseCore 0:
  337.6 208.5 reduce-scatter.1
  554.4 93.1 all-gather.1
